TPU v7x, 128 devices: a whole 4x4x4 slice. The times are simulated.
128 devices in a mesh: ty: 8 (over x, core), tx: 16 (over z, y).
Axes of the slice: x: 4, y: 4, z: 4, core: 2. Of those that a mesh axis runs over, the one named last changes fastest.
Arguments:
- exposures: float32 [1024, 128, 128], P(('ty', 'tx')), may hold values from -70 to 70
- point_spread: float32 [1024, 31, 31], P(('ty', 'tx')), may hold values from 0.0001 to 1
- warp_steps: int32 [1024, 2], P(('ty', 'tx')), may hold values from 0 to 3
- column: int32 [1024, 1], P(('ty', 'tx')), may hold values from 0 to 15; in each aligned block of 8 rows (0 to 7, 8 to 15, ...) at most 2 rows name the same one
- block_cell: int32 [1024], P(('ty', 'tx')), may hold values from 0 to 15
Outputs:
- solution: float32 [4096, 8192], P('ty', 'tx')
- residual: float32 [4096, 8192], P('ty', 'tx')
Inputs may be any that keep to these rules, and one draw needn't show every extreme that they name: `column`: among the 8 frame blocks of one device (aligned blocks of 8 rows) no value occurs more than 2 times, and in some such block one value occurs exactly 2 times.
All inputs are finite; a program needn't handle non-finite values.
Results may differ from a plain program's by a relative error of at most 0.0042.
Values may be sent and summed in bfloat16 or wider, within the bound.
No kernel may reach another device: no remote copies, remote signals or barrier semaphores. Data moves between devices by JAX's collectives and lax.ppermute only.
A program may use at most 192 MiB of HBM per device.

v0:
```python
import jax
import jax.numpy as jnp
from jax import lax
from jax.sharding import Mesh
from jax.sharding import PartitionSpec as P

TILE = 512
SUB = 4
ITERS = 2
TX = ("tx_0", "tx_1")
TY_TX = ("ty_0", "ty_1", "tx_0", "tx_1")
TY = ("ty_0", "ty_1")


damping = 0.05


def with_halo(value, sides, width):
    for axis, dim in sides:
        size, length = (lax.axis_size(axis), value.shape[dim])
        up = [(i, (i + 1) % size) for i in range(size - 1)]
        down = [(j, i) for i, j in up]
        last = lax.slice_in_dim(value, length - width, length, axis=dim)
        first = lax.slice_in_dim(value, 0, width, axis=dim)
        before = lax.ppermute(last, axis, up)
        after = lax.ppermute(first, axis, down)
        value = jnp.concatenate([before, value, after], axis=dim)
    return value


def over_axes(value, axes):
    for axis in axes:
        value = lax.psum(value, axis)
    return value


def make_kernels(point_spread, warp_steps):
    tap_count = point_spread.shape[-1] + 1
    totals = jnp.sum(point_spread, axis=(1, 2), keepdims=True)
    padded = jnp.pad(point_spread / totals, ((0, 0), (0, 1), (0, 1)))
    row_frac = (warp_steps[:, 0].astype(jnp.float32) / SUB)[:, None, None]
    col_frac = (warp_steps[:, 1].astype(jnp.float32) / SUB)[:, None, None]
    shifted = jnp.pad(padded, ((0, 0), (0, 0), (1, 0)))[:, :, :tap_count]
    blended = (1.0 - col_frac) * padded + col_frac * shifted
    lowered = jnp.pad(blended, ((0, 0), (1, 0), (0, 0)))[:, :tap_count, :]
    return ((1.0 - row_frac) * blended + row_frac * lowered).astype(jnp.bfloat16)


def tap_table(tap_count, block_side, window):
    taps_index = jnp.arange(tap_count)[:, None, None]
    positions = jnp.arange(window)[:, None]
    columns = jnp.arange(block_side)[None, :]
    forward_table = jnp.where(positions - columns == taps_index, 1.0, 0.0).astype(jnp.bfloat16)
    return forward_table.reshape(tap_count, window * block_side)


def build_bands(kernels, forward_table, block_side, window, tap_count):

    def one_band(kernel):
        banded = jnp.dot(kernel, forward_table, preferred_element_type=jnp.float32).astype(
            jnp.bfloat16
        )
        return banded.reshape(tap_count * window, block_side)

    return lax.map(one_band, kernels)


def forward_block(flat_window, banded, block_side, window, tap_count):
    framed = flat_window.reshape(window, window)
    stacked = jnp.concatenate(
        [framed[offset : offset + block_side] for offset in range(tap_count)], axis=1
    )
    return jnp.dot(stacked, banded, preferred_element_type=jnp.float32)


def adjoint_block(frame_image, banded, block_side, window, tap_count):
    spread = lax.dot_general(
        frame_image, banded, (((1,), (1,)), ((), ())), preferred_element_type=jnp.float32
    )
    spread = spread.reshape(block_side, tap_count, window)
    summed = jnp.zeros((window, window), jnp.float32)
    for offset in range(tap_count):
        summed = summed + jnp.pad(
            spread[:, offset, :], ((offset, window - block_side - offset), (0, 0))
        )
    return summed


def split_rows(values, block_side, margin, count):
    head = values[: count * block_side].reshape(count, block_side, -1)
    tail = jnp.pad(values[block_side:], ((0, block_side - 2 * margin), (0, 0)))
    tail = tail.reshape(count, block_side, -1)[:, : 2 * margin]
    return jnp.concatenate([head, tail], axis=1)


def fold_rows(pieces, block_side, margin, count):
    extent = count * block_side + 2 * margin
    head = pieces[:, :block_side].reshape(count * block_side, -1)
    tail = jnp.pad(pieces[:, block_side:], ((0, 0), (0, block_side - 2 * margin), (0, 0))).reshape(
        count * block_side, -1
    )
    return (
        jnp.pad(head, ((0, 2 * margin), (0, 0))) + jnp.pad(tail, ((block_side, 0), (0, 0)))[:extent]
    )


def fold_edges(values, axis_index, margin, extent):
    interior = lax.slice_in_dim(values, 2 * margin, 2 * margin + extent, axis=axis_index)
    lower_rim = lax.slice_in_dim(values, 0, margin, axis=axis_index)
    upper_rim = lax.slice_in_dim(values, extent + 3 * margin, extent + 4 * margin, axis=axis_index)
    widths_low = [(0, 0)] * values.ndim
    widths_high = [(0, 0)] * values.ndim
    widths_low[axis_index] = (0, extent - margin)
    widths_high[axis_index] = (extent - margin, 0)
    return interior + jnp.pad(lower_rim, widths_low) + jnp.pad(upper_rim, widths_high)


def body(exposures, point_spread, warp_steps, column, block_cell):
    frame_count = exposures.shape[0]
    block_side = exposures.shape[1]
    tap_count = point_spread.shape[1] + 1
    margin = tap_count // 2
    window = block_side + 2 * margin
    tx_size = lax.axis_size(TX)
    capacity = max(2, 2 * frame_count // tx_size)
    slot_count = tx_size * capacity
    per_row = TILE // block_side
    cell_count = per_row * per_row
    extent = TILE + 2 * margin
    kernels = make_kernels(point_spread, warp_steps)
    forward_table = tap_table(tap_count, block_side, window)
    target = column[:, 0]
    earlier = jnp.arange(frame_count)[:, None] > jnp.arange(frame_count)[None, :]
    matching = target[:, None] == target[None, :]
    standing = jnp.sum(jnp.where(earlier & matching, 1, 0), axis=1)
    slot_index = target * capacity + standing
    chosen = jnp.where(slot_index[None, :] == jnp.arange(slot_count)[:, None], 1, 0).astype(
        jnp.int32
    )
    chosen_low = chosen.astype(jnp.bfloat16)
    chosen_wide = chosen.astype(jnp.float32)
    request = jnp.sum(chosen * (block_cell + 1)[None, :], axis=1).reshape(tx_size, capacity)
    incoming = lax.all_to_all(request, TX, split_axis=0, concat_axis=0, tiled=True)
    wanted_cell = incoming.reshape(slot_count) - 1
    picking = wanted_cell[:, None] == jnp.arange(cell_count)[None, :]
    pick_low = jnp.where(picking, 1.0, 0.0).astype(jnp.bfloat16)
    pick_wide = jnp.where(picking, 1.0, 0.0).astype(jnp.float32)

    def spread_back(patches):
        cell_sums = jnp.dot(pick_wide.T, patches, precision=lax.Precision.HIGHEST)
        arranged = (
            cell_sums.reshape(per_row, per_row, window, window)
            .transpose(0, 2, 1, 3)
            .reshape(per_row, window, per_row * window)
        )
        row_folded = fold_rows(arranged, block_side, margin, per_row)
        turned = row_folded.reshape(extent, per_row, window).transpose(1, 2, 0)
        accumulated = fold_rows(turned, block_side, margin, per_row).T
        extended = with_halo(accumulated, ((TY, 0), (TX, 1)), margin)
        return fold_edges(fold_edges(extended, 0, margin, TILE), 1, margin, TILE)

    def apply_forward(operands):
        return forward_block(operands[0], operands[1], block_side, window, tap_count)

    def apply_back(operands):
        return adjoint_block(operands[0], operands[1], block_side, window, tap_count)

    frame_bands = build_bands(kernels, forward_table, block_side, window, tap_count)

    def adjoint_pass(images_low):
        patches = lax.map(apply_back, (images_low, frame_bands)).reshape(frame_count, -1)
        outgoing = jnp.dot(chosen_wide, patches, precision=lax.Precision.HIGHEST)
        returned = lax.all_to_all(
            outgoing.reshape(tx_size, capacity, -1), TX, split_axis=0, concat_axis=0, tiled=True
        )
        return spread_back(returned.reshape(slot_count, -1))

    first_images = exposures.astype(jnp.bfloat16)
    right_side = adjoint_pass(first_images)
    solution = jnp.zeros_like(right_side)
    residual = right_side
    direction = right_side
    norm_now = over_axes(jnp.sum(residual * residual), TY_TX)
    for iteration in range(ITERS):
        cut_extended = with_halo(direction.astype(jnp.bfloat16), ((TY, 0), (TX, 1)), margin)
        row_pieces = split_rows(cut_extended, block_side, margin, per_row)
        cut_turned = row_pieces.transpose(2, 0, 1).reshape(extent, per_row * window)
        both = split_rows(cut_turned, block_side, margin, per_row).reshape(
            per_row, window, per_row, window
        )
        cell_windows = both.transpose(2, 0, 3, 1).reshape(cell_count, window * window)
        pieces = (
            jnp.dot(pick_low, cell_windows, preferred_element_type=jnp.float32)
            .astype(jnp.bfloat16)
            .reshape(tx_size, capacity, -1)
        )
        arrived = lax.all_to_all(pieces, TX, split_axis=0, concat_axis=0, tiled=True).reshape(
            slot_count, -1
        )
        own_windows = jnp.dot(chosen_low.T, arrived, preferred_element_type=jnp.float32).astype(
            jnp.bfloat16
        )
        modelled = lax.map(apply_forward, (own_windows, frame_bands))
        applied = adjoint_pass(modelled.astype(jnp.bfloat16)) + damping * direction
        curvature, cross_term, square = (
            over_axes(jnp.sum(direction * applied), TY_TX),
            over_axes(jnp.sum(residual * applied), TY_TX),
            over_axes(jnp.sum(applied * applied), TY_TX),
        )
        step_size = norm_now / curvature
        solution = solution + step_size * direction
        residual = residual - step_size * applied
        if iteration + 1 < ITERS:
            norm_next = norm_now - 2.0 * step_size * cross_term + step_size * step_size * square
            direction = residual + norm_next / norm_now * direction
            norm_now = norm_next
    return (solution, residual)


def solution(mesh):
    torus = Mesh(mesh.devices.reshape(4, 2, 4, 4), ("ty_0", "ty_1", "tx_0", "tx_1"))
    in_specs = (
        P(TY_TX, None, None),
        P(TY_TX, None, None),
        P(TY_TX, None),
        P(TY_TX, None),
        P(TY_TX),
    )
    out_specs = (P(TY, TX), P(TY, TX))
    return jax.shard_map(body, mesh=torus, in_specs=in_specs, out_specs=out_specs, check_vma=False)
```

profile of v0, /device:TPU:0, one launch (start us, length us, event | category | flops | bytes accessed | tf_op | source)
XLA Modules:
  0.0 1207.6 jit_solution(3796065026061334829)
XLA Ops:
  3.0 8.1 all-to-all-start
  15.0 18.6 %while.72 = (s32[]{:T(128)}, bf16[8,5120,128]{2,1,0:T(8,128)(2,1)}, bf16[8,32,32]{2,1,0:T(8,128)(2,1)S(1)}, s32[20480]{0:T(1024)S(1)}, s32[]{:T(128)}) while((s32[]{:T(128)}, bf16[8,5120,128]{2,1,0:T(8,128)(2,1)}, bf16[8,32,32]{2,1,0:T(8,128)(2,1)S(1)}, s32[20480]{0:T(1024)S(1)}, s32[]{:T(128)}) %tuple.303), condition=%wide.region_4.5_spmd.clone, body=%wide.region_3.4_spmd.clone.sunk | while | flops 44564480 | bytes 6644289 | solution.py:65
  33.7 29.3 %while.67 = (s32[]{:T(128)}, f32[8,160,160]{2,1,0:T(8,128)S(1)}, bf16[8,128,128]{2,1,0:T(8,128)(2,1)S(1)}, bf16[8,5120,128]{2,1,0:T(8,128)(2,1)}, s32[]{:T(128)}) while((s32[]{:T(128)}, f32[8,160,160]{2,1,0:T(8,128)S(1)}, bf16[8,128,128]{2,1,0:T(8,128)(2,1)S(1)}, bf16[8,5120,128]{2,1,0:T(8,128)(2,1)}, s32[]{:T(128)}) %tuple.306), condition=%wide.region_6.7_spmd, body=%wide.region_5.6_spmd.sunk | while | flops 168565760 | bytes 15085641 | solution.py:171
  71.1 7.5 all-to-all-start.1
  78.7 47.6 %all-to-all-done.1 = f32[16,2,25600]{2,1,0:T(2,128)S(1)} async-done(((f32[16,2,25600]{2,1,0:T(2,128)}), f32[16,2,25600]{2,1,0:T(2,128)S(1)}, u32[]{:S(2)}, u32[]{:S(2)}) %all-to-all-start.1) | async-done | bytes 3276832 | tf_op jit(solution)/shard_map/all_to_all | solution.py:173
  129.8 6.0 dot_general.68
  135.9 9.0 fusion.51
  170.7 5.1 collective-permute-done.3
  190.3 4.8 collective-permute-done.7
  205.0 11.3 all-to-all-start.2
  216.3 28.8 %all-to-all-done.2 = bf16[16,2,25600]{2,1,0:T(2,128)(2,1)S(1)} async-done(((bf16[16,2,25600]{2,1,0:T(2,128)(2,1)}), bf16[16,2,25600]{2,1,0:T(2,128)(2,1)S(1)}, u32[]{:S(2)}, u32[]{:S(2)}) %all-to-all-start.2) | async-done | bytes 1638432 | tf_op jit(solution)/shard_map/all_to_all | solution.py:197
  249.2 251.4 %while.68 = (s32[]{:T(128)}, bf16[8,128,128]{2,1,0:T(8,128)(2,1)}, bf16[8,25600]{1,0:T(8,128)(2,1)S(1)}, bf16[8,5120,128]{2,1,0:T(8,128)(2,1)}, s32[]{:T(128)}, ...) while((s32[]{:T(128)}, bf16[8,128,128]{2,1,0:T(8,128)(2,1)}, ...), condition=%wide.region_13.14_spmd, body=%wide.region_12.13_spmd.sunk | while | flops 167772192 | bytes 10553141 | solution.py:203
  249.2 5.5 dynamic-slice_reduce_fusion.68
  280.6 5.5 dynamic-slice_reduce_fusion.68
  312.0 5.5 dynamic-slice_reduce_fusion.68
  343.4 5.5 dynamic-slice_reduce_fusion.68
  374.8 5.5 dynamic-slice_reduce_fusion.68
  406.2 5.5 dynamic-slice_reduce_fusion.68
  437.6 5.5 dynamic-slice_reduce_fusion.68
  469.0 5.5 dynamic-slice_reduce_fusion.68
  501.8 40.5 %while.69 = (s32[]{:T(128)}, f32[8,160,160]{2,1,0:T(8,128)}, bf16[8,128,128]{2,1,0:T(8,128)(2,1)}, bf16[8,5120,128]{2,1,0:T(8,128)(2,1)}, s32[]{:T(128)}) while((s32[]{:T(128)}, f32[8,160,160]{2,1,0:T(8,128)}, bf16[8,128,128]{2,1,0:T(8,128)(2,1)}, bf16[8,5120,128]{2,1,0:T(8,128)(2,1)}, s32[]{:T(128)}) %tuple.322), condition=%wide.region_15.16_spmd, body=%wide.region_14.15_spmd.sunk | while | flops 168565760 | bytes 15025217 | solution.py:171
  549.8 45.4 %all_to_all.34 = f32[16,2,25600]{2,1,0:T(2,128)} all-to-all(f32[16,2,25600]{2,1,0:T(2,128)S(1)} %copy.129), channel_id=1, replica_groups=mesh['ty_0'=4,'ty_1'=2,'tx_0'=4,'tx_1'=4] {'tx_0','tx_1'}, dimensions={0} | all-to-all | bytes 6553600 | tf_op jit(solution)/shard_map/all_to_all | solution.py:173
  595.2 4.9 reshape.374
  600.1 6.0 dot_general.74
  606.2 10.5 fusion.54
  656.5 9.9 all-reduce.129
  669.5 10.3 all-reduce.128
  679.8 11.9 all-reduce.127
  719.2 9.3 all-to-all-start.4
  728.4 28.7 %all-to-all-done.4 = bf16[16,2,25600]{2,1,0:T(2,128)(2,1)S(1)} async-done(((bf16[16,2,25600]{2,1,0:T(2,128)(2,1)}), bf16[16,2,25600]{2,1,0:T(2,128)(2,1)S(1)}, u32[]{:S(2)}, u32[]{:S(2)}) %all-to-all-start.4) | async-done | bytes 1638432 | tf_op jit(solution)/shard_map/all_to_all | solution.py:197
  761.2 251.5 %while.70 = (s32[]{:T(128)}, bf16[8,128,128]{2,1,0:T(8,128)(2,1)}, bf16[8,25600]{1,0:T(8,128)(2,1)S(1)}, bf16[8,5120,128]{2,1,0:T(8,128)(2,1)}, s32[]{:T(128)}, ...) while((s32[]{:T(128)}, bf16[8,128,128]{2,1,0:T(8,128)(2,1)}, ...), condition=%wide.region_27.28_spmd, body=%wide.region_26.27_spmd.sunk | while | flops 167772192 | bytes 10553141 | solution.py:203
  761.4 5.5 dynamic-slice_reduce_fusion.70
  792.8 5.5 dynamic-slice_reduce_fusion.70
  824.2 5.5 dynamic-slice_reduce_fusion.70
  855.5 5.5 dynamic-slice_reduce_fusion.70
  886.9 5.5 dynamic-slice_reduce_fusion.70
  918.3 5.5 dynamic-slice_reduce_fusion.70
  949.6 5.5 dynamic-slice_reduce_fusion.70
  981.0 5.5 dynamic-slice_reduce_fusion.70
  1014.0 40.5 %while.71 = (s32[]{:T(128)}, f32[8,160,160]{2,1,0:T(8,128)}, bf16[8,128,128]{2,1,0:T(8,128)(2,1)}, bf16[8,5120,128]{2,1,0:T(8,128)(2,1)}, s32[]{:T(128)}) while((s32[]{:T(128)}, f32[8,160,160]{2,1,0:T(8,128)}, bf16[8,128,128]{2,1,0:T(8,128)(2,1)}, bf16[8,5120,128]{2,1,0:T(8,128)(2,1)}, s32[]{:T(128)}) %tuple.324), condition=%wide.region_29.30_spmd, body=%wide.region_28.29_spmd.sunk | while | flops 168565760 | bytes 15025217 | solution.py:171
  1062.0 44.9 %all_to_all.35 = f32[16,2,25600]{2,1,0:T(2,128)} all-to-all(f32[16,2,25600]{2,1,0:T(2,128)S(1)} %copy.139), channel_id=1, replica_groups=mesh['ty_0'=4,'ty_1'=2,'tx_0'=4,'tx_1'=4] {'tx_0','tx_1'}, dimensions={0} | all-to-all | bytes 6553600 | tf_op jit(solution)/shard_map/all_to_all | solution.py:173
  1106.9 4.9 reshape.388
  1111.8 6.1 dot_general.80
  1117.9 10.5 fusion.57
  1155.4 5.1 collective-permute-done.18
  1168.2 10.7 psum.136
  1182.0 10.2 psum.138
  1192.1 11.5 psum.139
  (981 shorter events, 741.3 us)
Async XLA Ops:
  2.2 244.4 %copy-start.14 = (s32[8]{0:T(128)}, s32[8]{0:T(128)S(1)}, u32[]{:S(2)}) copy-start(s32[8]{0:T(128)S(1)} %get-tuple-element.500) | copy-start | bytes 100
  3.0 68.1 %all-to-all-start = ((s32[16,1,2]{2,1,0:T(1,128)}), s32[16,1,2]{2,1,0:T(1,128)S(1)}, u32[]{:S(2)}, u32[]{:S(2)}) async-start(s32[16,1,2]{2,1,0:T(1,128)} %bitcast.113), calls=%async_computation | async-start | bytes 16384 | tf_op jit(solution)/shard_map/all_to_all | solution.py:143
  12.7 51.2 %copy-start.20 = (s32[16,2]{0,1:T(2,128)}, s32[16,2]{0,1:T(2,128)S(1)}, u32[]{:S(2)}) copy-start(s32[16,2]{0,1:T(2,128)S(1)} %multiply_add_fusion.4) | copy-start | bytes 388
  15.0 18.6 %copy-start.7 = (f32[8,128,128]{2,1,0:T(8,128)S(1)}, f32[8,128,128]{2,1,0:T(8,128)}, u32[]{:S(2)}) copy-start(f32[8,128,128]{2,1,0:T(8,128)} %param.17) | copy-start | bytes 1572868
  71.1 55.3 %all-to-all-start.1 = ((f32[16,2,25600]{2,1,0:T(2,128)}), f32[16,2,25600]{2,1,0:T(2,128)S(1)}, u32[]{:S(2)}, u32[]{:S(2)}) async-start(f32[16,2,25600]{2,1,0:T(2,128)} %copy.119), calls=%async_computation.1 | async-start | bytes 6553600 | tf_op jit(solution)/shard_map/all_to_all | solution.py:173
  78.6 57.3 %copy-start.8 = (s32[4,4]{1,0:T(4,128)}, s32[4,4]{1,0:T(4,128)S(1)}, u32[]{:S(2)}) copy-start(s32[4,4]{1,0:T(4,128)S(1)} %multiply_add_fusion.3) | copy-start | bytes 196
  78.7 123.0 %copy-start.17 = (s32[32]{0:T(128)}, s32[32]{0:T(128)S(1)}, u32[]{:S(2)}) copy-start(s32[32]{0:T(128)S(1)} %sub.52) | copy-start | bytes 388
  149.6 1.8 slice-start.1
  156.0 1.2 copy-start.6
  157.5 2.6 collective-permute-start
  158.8 5.2 collective-permute-start.1
  164.1 6.6 collective-permute-start.2
  165.4 10.9 copy-start.11
  165.4 10.4 collective-permute-start.3
  177.1 4.8 collective-permute-start.4
  180.6 5.0 collective-permute-start.5
  185.8 4.5 collective-permute-start.6
  187.7 7.4 collective-permute-start.7
  205.0 40.1 %all-to-all-start.2 = ((bf16[16,2,25600]{2,1,0:T(2,128)(2,1)}), bf16[16,2,25600]{2,1,0:T(2,128)(2,1)S(1)}, u32[]{:S(2)}, u32[]{:S(2)}) async-start(bf16[16,2,25600]{2,1,0:T(2,128)(2,1)} %reshape.371), calls=%async_computation.2 | async-start | bytes 3276800 | tf_op jit(solution)/shard_map/all_to_all | solution.py:197
  542.2 2.2 copy-start.15
  542.2 2.2 copy-start.21
  600.1 6.0 copy-start.9
  600.1 6.0 copy-start.18
  619.6 1.2 copy-start.2
  621.9 3.0 slice-start.2
  635.4 2.6 collective-permute-start.8
  636.7 4.8 collective-permute-start.9
  641.7 8.1 collective-permute-start.10
  644.2 10.8 copy-start.12
  644.2 10.3 collective-permute-start.11
  656.5 44.5 %copy-start = (f32[512,512]{1,0:T(8,128)}, f32[512,512]{1,0:T(8,128)S(1)}, u32[]{:S(2)}) copy-start(f32[512,512]{1,0:T(8,128)S(1)} %get-tuple-element.375) | copy-start | bytes 3145732
  696.0 2.6 collective-permute-start.12
  697.3 3.6 collective-permute-start.13
  701.0 3.9 collective-permute-start.14
  702.3 6.9 collective-permute-start.15
  719.2 38.0 %all-to-all-start.4 = ((bf16[16,2,25600]{2,1,0:T(2,128)(2,1)}), bf16[16,2,25600]{2,1,0:T(2,128)(2,1)S(1)}, u32[]{:S(2)}, u32[]{:S(2)}) async-start(bf16[16,2,25600]{2,1,0:T(2,128)(2,1)} %reshape.385), calls=%async_computation.4 | async-start | bytes 3276800 | tf_op jit(solution)/shard_map/all_to_all | solution.py:197
  1054.4 2.2 copy-start.16
  1054.4 2.2 copy-start.22
  1111.8 6.1 copy-start.10
  1111.8 6.1 copy-start.19
  1131.4 1.2 copy-start.3
  1133.8 2.9 slice-start.3
  1147.1 2.6 collective-permute-start.16
  1148.4 3.1 collective-permute-start.17
  1151.6 8.9 collective-permute-start.18
  1154.1 11.7 copy-start.13
  1154.1 11.1 collective-permute-start.19
  1165.8 1.2 copy-start.1
  (5 other events, 4.9 us)
where the time goes:
time: 1220 us; the launch traced here: 1210 us
  local copies, waits for them, and re-layouts  638 us (52%)
  blocking collectives  161 us (13%)
  waiting for transfers between devices  159 us (13%)
  matrix products  113 us (9%)
  starting transfers between devices  68.1 us (6%)
  other arithmetic  59.2 us (5%)
    slice x544, local copies, waits for them, and re-layouts, forward_block(): framed[offset:offset + block_side]  416 us
    all_to_all x2, blocking collectives, adjoint_pass(): lax.all_to_all(outgoing.reshape(tx_size, capacity, -1), TX, split_axis=0,...  90.3 us
    psum x8, blocking collectives, over_axes(): value = lax.psum(value, axis)  70.6 us
    all_to_all x2, waiting for transfers between devices, body(): lax.all_to_all(pieces, TX, split_axis=0, concat_axis=0, tiled=True)  57.5 us
    all_to_all x1, waiting for transfers between devices, adjoint_pass(): lax.all_to_all(outgoing.reshape(tx_size, capacity, -1), TX, split_axis=0,...  47.6 us
    concatenate x16, local copies, waits for them, and re-layouts, forward_block(): jnp.concatenate([framed[offset:offset + block_side] for offset in range(t...  46.5 us
    ppermute x10, waiting for transfers between devices, with_halo(): after = lax.ppermute(first, axis, down)  38.9 us
    dot_general x16, matrix products, forward_block(): return jnp.dot(stacked, banded, preferred_element_type=jnp.float32)  38.9 us
  transfers between devices with their start and end apart: 24, of which 18 were waited for; matrix products, arithmetic and copies ran while one was open for 5% of the time, Pallas kernels for 0%

commit v1 on v0

v1 whole, which is shorter than its diff:
```python
import functools

import jax
import jax.numpy as jnp
from jax import lax
from jax.experimental import pallas as pl
from jax.experimental.pallas import tpu as pltpu
from jax.sharding import Mesh
from jax.sharding import PartitionSpec as P

TX = ("tx_0", "tx_1")
TY = ("ty_0", "ty_1")
TY_TX = TY + TX
N_TY, N_TX = 8, 16

SUB = 4
DAMPING = 0.05
FB = 8
CAP = 2
SLOTS = N_TX * CAP
TILE, BLOCK, HALO, TAPS, PSF = 512, 128, 16, 32, 31
EXT = TILE + 2 * HALO
LANES = 640
RIM = 2 * HALO
WIN = BLOCK + 2 * HALO
SLOT_ROWS = 160
F32, BF16 = jnp.float32, jnp.bfloat16
VMEM_BYTES = 48 << 20


def iota(shape, axis):
    return lax.broadcasted_iota(jnp.int32, shape, axis)


def by_group(lane, parts):
    low = jnp.where(lane < 32, parts[0], parts[1])
    high = jnp.where(lane < 96, parts[2], parts[3])
    return jnp.where(lane < 64, low, high)


def pack_kernel(column, cell, warp, spread_ref, exposures_ref, out_ref, pad, kern):
    pad[...] = jnp.zeros_like(pad)
    for f in range(FB):
        pad[f, 0:PSF, 0:PSF] = spread_ref[f]
    for f in range(FB):
        point = pad[f]
        point = point / jnp.sum(point, keepdims=True)
        row_frac = warp[f, 0].astype(F32) / SUB
        col_frac = warp[f, 1].astype(F32) / SUB
        blended = (1.0 - col_frac) * point + col_frac * pltpu.roll(point, 1, 1)
        lowered = pltpu.roll(blended, 1, 0)
        kern[32 * f : 32 * f + 32, :] = (
            (1.0 - row_frac) * blended + row_frac * lowered
        ).astype(BF16)
    row, lane = iota((128, 128), 0), iota((128, 128), 1)
    tall, wide = iota((32 * FB, 128), 0), iota((32 * FB, 128), 1)
    tap = tall & 31
    place = jnp.where((lane & 31) == 31 - row, 1.0, 0.0).astype(BF16)
    spread = jnp.dot(kern[...], place, preferred_element_type=F32)
    spread = jnp.where((wide >> 5) == ((tap >> 2) & 3), spread, 0.0).astype(BF16)
    target, source = iota((8 * FB, 32 * FB), 0), iota((8 * FB, 32 * FB), 1)
    s_tap = source & 31
    pick = ((source >> 5) == (target >> 3)) & (
        (target & 7) == 2 * (s_tap & 3) + (s_tap >> 4)
    )
    backward = jnp.dot(
        jnp.where(pick, 1.0, 0.0).astype(BF16), spread, preferred_element_type=F32
    )
    place = jnp.where((lane & 63) == row, 1.0, 0.0).astype(BF16)
    spread = jnp.dot(kern[...], place, preferred_element_type=F32)
    spread = jnp.where((wide >> 6) == (tap & 1), spread, 0.0).astype(BF16)
    target, source = iota((16 * FB, 32 * FB), 0), iota((16 * FB, 32 * FB), 1)
    pick = ((source >> 5) == (target >> 4)) & ((target & 15) == ((source & 31) >> 1))
    ahead = jnp.dot(
        jnp.where(pick, 1.0, 0.0).astype(BF16), spread, preferred_element_type=F32
    )
    for s in range(SLOTS):
        out_ref[s, 128:SLOT_ROWS, :] = jnp.zeros((SLOT_ROWS - 128, 128), BF16)
    for f in range(FB):
        standing = jnp.int32(0)
        for g in range(f):
            standing = standing + jnp.where(column[g] == column[f], 1, 0)
        slot = CAP * column[f] + jnp.minimum(standing, CAP - 1)
        out_ref[slot, 0:BLOCK, :] = exposures_ref[f].astype(BF16)
        tail = jnp.concatenate(
            [
                backward[8 * f : 8 * f + 8],
                ahead[16 * f : 16 * f + 16],
                jnp.broadcast_to((cell[f] + 1).astype(F32), (8, 128)),
            ],
            axis=0,
        )
        out_ref[slot, 128:SLOT_ROWS, :] = tail.astype(BF16)


def pack(column, cell, warp, spread, exposures):
    smem = pl.BlockSpec(memory_space=pltpu.SMEM)
    vmem = pl.BlockSpec(memory_space=pltpu.VMEM)
    return pl.pallas_call(
        pack_kernel,
        out_shape=jax.ShapeDtypeStruct((SLOTS, SLOT_ROWS, 128), BF16),
        in_specs=[smem, smem, smem, vmem, vmem],
        out_specs=vmem,
        scratch_shapes=[pltpu.VMEM((FB, 32, 128), F32), pltpu.VMEM((32 * FB, 128), BF16)],
        compiler_params=pltpu.CompilerParams(vmem_limit_bytes=VMEM_BYTES),
        name="pack",
    )(column, cell, warp, spread, exposures)


def list_frames(cells, frames):
    count = jnp.int32(0)
    for s in range(SLOTS):
        frames[count] = s
        count = count + jnp.where(cells[s] > 0, 1, 0)
    return count


def build_taps(taps, taps_out):
    row, lane = iota((64, 128), 0), iota((64, 128), 1)
    offset = (lane & 31) + 31 - row
    inside = (offset >= 0) & (offset < 32)
    for a2 in range(4):
        for h in range(2):
            line = jnp.broadcast_to(taps[2 * a2 + h : 2 * a2 + h + 1], (64, 128))
            line = pltpu.roll(line, 97, 1, stride=1, stride_axis=0)
            taps_out[0, 64 * a2 : 64 * a2 + 64, 128 * h : 128 * h + 128] = jnp.where(
                inside, line, 0.0
            ).astype(BF16)
    for a1 in range(8):
        for half in range(2):
            at = 8 + 2 * a1 + half
            line = jnp.broadcast_to(taps[at : at + 1], (32, 128))
            line = pltpu.roll(line, 0, 1, stride=1, stride_axis=0)
            taps_out[1, 32 * a1 : 32 * a1 + 32, 128 * half : 128 * half + 128] = line.astype(
                BF16
            )


def unfold(field, doubled, stack):
    rows = 32

    def columns(at, carry):
        left = pl.ds(pl.multiple_of(128 * at, 128), 128)
        right = pl.ds(pl.multiple_of(128 * at + 128, 128), 128)
        for r in range(0, EXT + 8, 24):
            lane = iota((24, 128), 1)
            here, there = field[r : r + 24, left], field[r : r + 24, right]
            turned = pltpu.roll(here, 64, 1)
            odd = pltpu.roll(here, 96, 1)
            odd_turned = pltpu.roll(odd, 64, 1)
            last = jnp.where(lane < 96, odd, pltpu.roll(there, 96, 1))
            last_turned = pltpu.roll(last, 64, 1)
            doubled[0, r : r + 24] = jnp.where(lane < 64, here, turned)
            doubled[1, r : r + 24] = jnp.where(lane < 64, odd, odd_turned)
            doubled[2, r : r + 24] = jnp.where(lane < 64, turned, here)
            doubled[3, r : r + 24] = jnp.where(lane < 64, last_turned, last)
        lane = iota((rows, 128), 1)
        for k in range(4):
            for r in range(0, EXT, rows):
                part = [doubled[k, r + a : r + a + rows] for a in range(4)]
                stack[4 * at + k, r : r + rows, 0:128] = jnp.where(
                    lane < 64, part[0], part[1]
                ).astype(BF16)
                stack[4 * at + k, r : r + rows, 128:256] = jnp.where(
                    lane < 64, part[2], part[3]
                ).astype(BF16)
        return carry

    lax.fori_loop(0, TILE // 128, columns, 0)


def fold(total, field):
    rows = 32
    lane = iota((rows, 128), 1)

    def block(b, r):
        even = total[b, r + 8 : r + 8 + rows, 0:128] + total[b, r + 6 : r + 6 + rows, 128:256]
        odd = total[b, r + 7 : r + 7 + rows, 0:128] + total[b, r + 5 : r + 5 + rows, 128:256]
        return jnp.where(lane < 64, even, odd)

    def columns(at, carry):
        here = pl.ds(pl.multiple_of(128 * at, 128), 128)
        for r in range(0, EXT, rows):
            before = block(4 * at, r)
            b0, b1, b2, b3 = [block(4 * at + 1 + k, r) for k in range(4)]
            even = jnp.where(lane < 64, b0, b2) + pltpu.roll(jnp.where(lane < 64, b2, b0), 64, 1)
            direct = jnp.where(lane < 64, b1, jnp.where(lane < 96, b3, before))
            turned = jnp.where(lane < 64, jnp.where(lane < 32, b3, before), b1)
            odd = direct + pltpu.roll(turned, 64, 1)
            field[r : r + rows, here] = even + pltpu.roll(odd, 32, 1)
        return carry

    lax.fori_loop(0, TILE // 128, columns, 0)
    for r in range(0, EXT, rows):
        before = block(TILE // 32, r)
        before = pltpu.roll(before + pltpu.roll(before, 64, 1), 32, 1)
        field[r : r + rows, TILE:LANES] = jnp.where(lane < RIM, before, 0.0)


def clear_total(total):
    def clear(b, carry):
        total[b] = jnp.zeros(total.shape[1:], F32)
        return carry

    lax.fori_loop(0, total.shape[0], clear, 0)


def expand_and_add(image_chunks, turned, spread, taps, total, lx, top):
    for c in range(4):
        for d in range(4):
            moved = image_chunks[c] if d == 0 else pltpu.roll(image_chunks[c], 32 * d, 1)
            turned[d, 16 + 32 * c : 48 + 32 * c] = moved
    lane = iota((48, 128), 1)
    for xb in range(4):
        for q in range(0, 144, 48):
            parts = [turned[(j - xb) % 4, 16 - 4 * j + q : 64 - 4 * j + q] for j in range(4)]
            spread[xb, 16 + q : 64 + q] = by_group(lane, parts).astype(BF16)
    both = jnp.concatenate([spread[:, 16:176], spread[:, 0:160]], axis=2).reshape(640, 256)
    window = jnp.dot(both, taps, preferred_element_type=F32).reshape(4, WIN, 256)
    at = pl.ds(pl.multiple_of(8 + top, 8), WIN)
    total[pl.ds(1 + lx, 4), at, :] += window


def clear_margins(turned, spread):
    turned[:, 0:16] = jnp.zeros((4, 16, 128), F32)
    turned[:, 144:160] = jnp.zeros((4, 16, 128), F32)
    spread[:, 0:16] = jnp.zeros((4, 16, 128), BF16)
    spread[:, 160:176] = jnp.zeros((4, 16, 128), BF16)


def write_rims(field, left_ref, right_ref, top_ref, bottom_ref):
    left_ref[...] = jnp.zeros_like(left_ref)
    right_ref[...] = jnp.zeros_like(right_ref)
    for r in range(0, TILE, 128):
        left_ref[:, r : r + 128] = field[r : r + 128, 0:128].T[0:RIM]
        right_ref[:, r : r + 128] = field[r : r + 128, TILE : TILE + 128].T[0:RIM]
    left_ref[:, TILE:EXT] = field[TILE:EXT, 0:128].T[0:RIM]
    right_ref[:, TILE:EXT] = field[TILE:EXT, TILE : TILE + 128].T[0:RIM]
    top_ref[...] = field[0:RIM, :]
    bottom_ref[...] = field[TILE:EXT, :]


def complete(place, own, rims, field):
    from_left, from_right, from_above, from_below = rims
    field[0:EXT, :] = own[...]
    field[EXT:, :] = jnp.zeros((field.shape[0] - EXT, LANES), F32)
    for r in range(0, TILE, 128):
        field[r : r + 128, 0:RIM] += from_left[:, r : r + 128].T
        field[r : r + 128, TILE:EXT] += from_right[:, r : r + 128].T
    field[TILE:EXT, 0:RIM] += from_left[:, TILE:LANES].T[0:RIM]
    field[TILE:EXT, TILE:EXT] += from_right[:, TILE:LANES].T[0:RIM]
    field[0:RIM, :] += from_above[...]
    field[TILE:EXT, :] += from_below[...]

    @pl.when(place[0] == 0)
    def _():
        field[0:HALO, :] = jnp.zeros((HALO, LANES), F32)

    @pl.when(place[0] == N_TY - 1)
    def _():
        field[EXT - HALO : EXT, :] = jnp.zeros((HALO, LANES), F32)

    @pl.when(place[1] == 0)
    def _():
        field[0:EXT, 0:HALO] = jnp.zeros((EXT, HALO), F32)

    @pl.when(place[1] == N_TX - 1)
    def _():
        field[0:EXT, EXT - HALO : EXT] = jnp.zeros((EXT, HALO), F32)


def inner_sum(chunk_of):
    sums = jnp.zeros((1, 128), F32)
    lane = iota((32, LANES), 1)
    inside = (lane >= HALO) & (lane < HALO + TILE)
    for r in range(HALO, HALO + TILE, 32):
        chunk = jnp.where(inside, chunk_of(r, 32), 0.0)
        by_lane = jnp.sum(chunk, axis=0, keepdims=True)
        for x in range(0, LANES, 128):
            sums = sums + by_lane[:, x : x + 128]
    return sums


def first_kernel(
    cells, slots_ref, own_ref, left_ref, right_ref, top_ref, bottom_ref, taps_out,
    frames, taps, total, turned, spread, sems,
):
    count = list_frames(cells, frames)
    clear_total(total)
    clear_margins(turned, spread)

    def frame(i, carry):
        s = frames[i]
        cell = cells[s] - 1
        lx, top = 4 * (cell & 3), BLOCK * (cell >> 2)
        build_taps(slots_ref[s, 128:SLOT_ROWS].astype(F32), taps.at[i])
        pltpu.make_async_copy(taps.at[i], taps_out.at[i], sems.at[i]).start()
        chunks = [slots_ref[s, r : r + 32].astype(F32) for r in range(0, BLOCK, 32)]
        expand_and_add(chunks, turned, spread, taps[i, 1], total, lx, top)
        return carry

    lax.fori_loop(0, count, frame, 0)
    fold(total, own_ref)
    write_rims(own_ref, left_ref, right_ref, top_ref, bottom_ref)

    def wait(i, carry):
        pltpu.make_async_copy(taps.at[i], taps_out.at[i], sems.at[i]).wait()
        return carry

    lax.fori_loop(0, count, wait, 0)


def frame_pass(cells, frames, count, taps_in, field, scratch):
    taps, total, turned, spread, stack, doubled, product, paired, sems = scratch
    unfold(field, doubled, stack)
    clear_total(total)
    clear_margins(turned, spread)

    def frame(i, sums):
        cell = cells[frames[i]] - 1
        lx, top = 4 * (cell & 3), BLOCK * (cell >> 2)
        pltpu.make_async_copy(taps_in.at[i], taps.at[i], sems.at[i]).wait()
        window = stack[pl.ds(lx, 4), pl.ds(pl.multiple_of(top, 128), WIN), :]
        product[...] = jnp.dot(
            window.reshape(4 * WIN, 256), taps[i, 0], preferred_element_type=F32
        ).reshape(4, WIN, 256)
        for xb in range(4):
            paired[xb] = product[xb, 0:144, 0:128] + product[xb, 16:160, 128:256]
        lane = iota((32, 128), 1)
        chunks = []
        for r in range(0, BLOCK, 32):
            modelled = None
            for d in range(4):
                parts = [paired[(j + d) % 4, r + 4 * j : r + 4 * j + 32] for j in range(4)]
                moved = by_group(lane, parts)
                moved = moved if d == 0 else pltpu.roll(moved, 32 * d, 1)
                modelled = moved if d == 0 else modelled + moved
            low = modelled.astype(BF16).astype(F32)
            sums = sums + jnp.sum(modelled * low, axis=0, keepdims=True)
            chunks.append(low)
        expand_and_add(chunks, turned, spread, taps[i, 1], total, lx, top)
        return sums

    return lax.fori_loop(0, count, frame, jnp.zeros((1, 128), F32))


def start_taps(cells, frames, taps_in, taps, sems):
    count = list_frames(cells, frames)

    def start(i, carry):
        pltpu.make_async_copy(taps_in.at[i], taps.at[i], sems.at[i]).start()
        return carry

    lax.fori_loop(0, count, start, 0)
    return count


def second_kernel(
    cells, place, own_in, rim_l, rim_r, rim_a, rim_b, taps_in,
    own_ref, left_ref, right_ref, top_ref, bottom_ref, residual_ref, sums_ref,
    frames, field, *scratch,
):
    count = start_taps(cells, frames, taps_in, scratch[0], scratch[-1])
    complete(place, own_in, (rim_l, rim_r, rim_a, rim_b), field)
    residual_ref[...] = field[0:EXT, :]
    square = inner_sum(lambda r, n: field[r : r + n, :] * field[r : r + n, :])
    curve = frame_pass(cells, frames, count, taps_in, field, scratch)
    fold(scratch[1], own_ref)
    write_rims(own_ref, left_ref, right_ref, top_ref, bottom_ref)
    sums_ref[...] = jnp.zeros_like(sums_ref)
    sums_ref[0:1] = square
    sums_ref[1:2] = curve


def first_step(sums):
    square = jnp.sum(sums[0:1], axis=1, keepdims=True)
    curve = jnp.sum(sums[1:2], axis=1, keepdims=True) + DAMPING * square
    return square, curve, square / curve


def third_kernel(
    cells, place, sums_in, own_in, rim_l, rim_r, rim_a, rim_b, start_ref, taps_in,
    own_ref, left_ref, right_ref, top_ref, bottom_ref, residual_ref, applied_ref, sums_ref,
    frames, field, *scratch,
):
    count = start_taps(cells, frames, taps_in, scratch[0], scratch[-1])
    complete(place, own_in, (rim_l, rim_r, rim_a, rim_b), field)
    step = first_step(sums_in[...])[2]
    for r in range(0, EXT, 32):
        start = start_ref[r : r + 32]
        applied = field[r : r + 32, :] + DAMPING * start
        residual = start - step * applied
        applied_ref[r : r + 32] = applied
        residual_ref[r : r + 32] = residual
        field[r : r + 32, :] = residual
    square = inner_sum(lambda r, n: field[r : r + n, :] * field[r : r + n, :])
    cross = inner_sum(lambda r, n: field[r : r + n, :] * applied_ref[r : r + n, :])
    curve = frame_pass(cells, frames, count, taps_in, field, scratch)
    fold(scratch[1], own_ref)
    write_rims(own_ref, left_ref, right_ref, top_ref, bottom_ref)
    sums_ref[...] = jnp.zeros_like(sums_ref)
    sums_ref[0:1] = square
    sums_ref[1:2] = cross
    sums_ref[2:3] = curve


def last_kernel(
    place, sums_one, sums_two, own_in, rim_l, rim_r, rim_a, rim_b, start_ref, applied_ref,
    residual_ref, solution_out, residual_out, field,
):
    complete(place, own_in, (rim_l, rim_r, rim_a, rim_b), field)
    square_one, curve_one, step_one = first_step(sums_one[...])
    sums = sums_two[...]
    square_two = jnp.sum(sums[0:1], axis=1, keepdims=True)
    cross = jnp.sum(sums[1:2], axis=1, keepdims=True)
    curve = jnp.sum(sums[2:3], axis=1, keepdims=True) + DAMPING * square_two
    ratio = square_two / square_one
    curve_two = curve + 2.0 * ratio * cross + ratio * ratio * curve_one
    step_two = square_two / curve_two
    lane = iota((32, 128), 1)
    for r in range(0, TILE, 32):
        rows = slice(r + HALO, r + HALO + 32)
        start, residual = start_ref[rows], residual_ref[rows]
        applied = field[rows, :] + DAMPING * residual + ratio * applied_ref[rows]
        total = step_one * start + step_two * (residual + ratio * start)
        left = residual - step_two * applied
        for value, out in ((total, solution_out), (left, residual_out)):
            parts = [
                pltpu.roll(value[:, x : x + 128], 128 - HALO, 1) for x in range(0, LANES, 128)
            ]
            for x in range(TILE // 128):
                out[r : r + 32, 128 * x : 128 * x + 128] = jnp.where(
                    lane < 128 - HALO, parts[x], parts[x + 1]
                )


def corner_kernel(top_ref, bottom_ref, from_left, from_right, top_out, bottom_out):
    top_out[...] = top_ref[...]
    bottom_out[...] = bottom_ref[...]
    for rim, at in ((from_left, 0), (from_right, TILE)):
        top_out[:, at : at + RIM] += rim[:, 0:128].T[0:RIM]
        bottom_out[:, at : at + RIM] += rim[:, TILE:LANES].T[0:RIM]


def call(kernel, outs, spaces, operands, scratch, name, out_spaces=None):
    specs = {
        "s": pl.BlockSpec(memory_space=pltpu.SMEM),
        "v": pl.BlockSpec(memory_space=pltpu.VMEM),
        "a": pl.BlockSpec(memory_space=pl.ANY),
    }
    return pl.pallas_call(
        kernel,
        out_shape=[jax.ShapeDtypeStruct(shape, kind) for shape, kind in outs],
        in_specs=[specs[space] for space in spaces],
        out_specs=[specs[space] for space in (out_spaces or "v" * len(outs))],
        scratch_shapes=scratch,
        compiler_params=pltpu.CompilerParams(vmem_limit_bytes=VMEM_BYTES),
        name=name,
    )(*operands)


FIELD = ((EXT, LANES), F32)
RIM_ARRAY = ((RIM, LANES), F32)
SUMS = ((8, 128), F32)
FRAME_LIST = pltpu.SMEM((SLOTS + 1,), jnp.int32)
TAPS_SCRATCH = pltpu.VMEM((SLOTS, 2, 256, 256), BF16)
TOTAL = pltpu.VMEM((TILE // 32 + 1, 8 + EXT, 256), F32)
TURNED = pltpu.VMEM((4, WIN, 128), F32)
SPREAD = pltpu.VMEM((4, WIN + 16, 128), BF16)
FIELD_SCRATCH = pltpu.VMEM((EXT + 8, LANES), F32)
PASS_SCRATCH = [
    FRAME_LIST,
    FIELD_SCRATCH,
    TAPS_SCRATCH,
    TOTAL,
    TURNED,
    SPREAD,
    pltpu.VMEM((TILE // 32, EXT, 256), BF16),
    pltpu.VMEM((4, EXT + 8, 128), F32),
    pltpu.VMEM((4, WIN, 256), F32),
    pltpu.VMEM((4, 144, 128), F32),
    pltpu.SemaphoreType.DMA((SLOTS,)),
]


def shift(value, axes, size, step):
    pairs = [(i, i + step) for i in range(size) if 0 <= i + step < size]
    return lax.ppermute(value, axes, pairs)


def trade_rims(left, right, top, bottom):
    from_left = shift(right, TX, N_TX, 1)
    from_right = shift(left, TX, N_TX, -1)
    top, bottom = call(
        corner_kernel,
        [RIM_ARRAY, RIM_ARRAY],
        "vvvv",
        (top, bottom, from_left, from_right),
        [],
        "corners",
    )
    from_above = shift(bottom, TY, N_TY, 1)
    from_below = shift(top, TY, N_TY, -1)
    return from_left, from_right, from_above, from_below


def total_sum(value):
    value = value + lax.ppermute(value, "ty_1", [(0, 1), (1, 0)])
    for axis in ("tx_1", "tx_0", "ty_0"):
        value = value + lax.ppermute(value, axis, [(0, 1), (1, 0), (2, 3), (3, 2)])
        value = value + lax.ppermute(value, axis, [(1, 2), (2, 1), (3, 0), (0, 3)])
    return value


def body(exposures, point_spread, warp_steps, column, block_cell):
    place = jnp.stack([lax.axis_index(TY), lax.axis_index(TX)]).astype(jnp.int32)
    sent = pack(column[:, 0], block_cell, warp_steps, point_spread, exposures)
    slots = lax.all_to_all(
        sent.reshape(N_TX, CAP, SLOT_ROWS, 128), TX, split_axis=0, concat_axis=0, tiled=True
    ).reshape(SLOTS, SLOT_ROWS, 128)
    cells = slots[:, SLOT_ROWS - 8, 0].astype(jnp.int32)
    rims_out = [RIM_ARRAY] * 4

    own, left, right, top, bottom, taps = call(
        first_kernel,
        [FIELD] + rims_out + [((SLOTS, 2, 256, 256), BF16)],
        "sv",
        (cells, slots),
        [FRAME_LIST, TAPS_SCRATCH, TOTAL, TURNED, SPREAD, pltpu.SemaphoreType.DMA((SLOTS,))],
        "right_side",
        "vvvvva",
    )
    rims = trade_rims(left, right, top, bottom)
    own, left, right, top, bottom, start, sums_one = call(
        second_kernel,
        [FIELD] + rims_out + [FIELD, SUMS],
        "ssvvvvva",
        (cells, place, own, *rims, taps),
        PASS_SCRATCH,
        "first_pass",
    )
    rims = trade_rims(left, right, top, bottom)
    sums_one = total_sum(sums_one)
    own, left, right, top, bottom, residual, applied, sums_two = call(
        third_kernel,
        [FIELD] + rims_out + [FIELD, FIELD, SUMS],
        "ssvvvvvvva",
        (cells, place, sums_one, own, *rims, start, taps),
        PASS_SCRATCH,
        "second_pass",
    )
    rims = trade_rims(left, right, top, bottom)
    sums_two = total_sum(sums_two)
    tile = ((TILE, TILE), F32)
    return tuple(
        call(
            last_kernel,
            [tile, tile],
            "svvvvvvvvvv",
            (place, sums_one, sums_two, own, *rims, start, applied, residual),
            [FIELD_SCRATCH],
            "finish",
        )
    )


def solution(mesh):
    torus = Mesh(mesh.devices.reshape(4, 2, 4, 4), TY_TX)
    in_specs = (
        P(TY_TX, None, None),
        P(TY_TX, None, None),
        P(TY_TX, None),
        P(TY_TX, None),
        P(TY_TX),
    )
    out_specs = (P(TY, TX), P(TY, TX))
    return jax.shard_map(body, mesh=torus, in_specs=in_specs, out_specs=out_specs, check_vma=False)
```

time: 1220 us -> 233 us (0.19)
  local copies, waits for them, and re-layouts: 638 us -> 6.23 us
  blocking collectives: 161 us -> 27.9 us
  matrix products: 113 us -> 0 us
  waiting for transfers between devices: 159 us -> 46.6 us
  other arithmetic: 59.2 us -> 0.78 us
  Pallas kernels: 0 us -> 54.5 us
  starting transfers between devices: 68.1 us -> 95.6 us
    slice x584 -> x0, local copies, waits for them, and re-layouts: 420 us -> none  [the longest x544 416 us: forward_block(): framed[offset:offset + block_side]]
    dot_general x58 -> x0, matrix products: 113 us -> none  [the longest x16 38.9 us: forward_block(): return jnp.dot(stacked, banded, preferred_element_type=jnp.float32)]
    all_to_all x4 -> x0, waiting for transfers between devices: 105 us -> none  [the longest x2 57.5 us: body(): lax.all_to_all(pieces, TX, split_axis=0, concat_axis=0, tiled=True)]
    psum x8 -> x0, blocking collectives: 70.6 us -> none  [over_axes(): value = lax.psum(value, axis)]
    ppermute x20 -> x26, starting transfers between devices: 31.9 us -> 95.6 us  [the longest x6 47.7 us: total_sum(): value = value + lax.ppermute(value, axis, [(1, 2), (2, 1), (3, 0), (0, 3)])]
    all_to_all x2 -> x1, blocking collectives: 90.3 us -> 27.9 us  [body(): lax.all_to_all(sent.reshape(N_TX, CAP, SLOT_ROWS, 128), TX, split_axis=0,...]
    reshape x27 -> x0, local copies, waits for them, and re-layouts: 60.5 us -> none  [the longest x6 14.5 us: fold_rows(): jnp.pad(pieces[:, block_side:], ((0, 0), (0, block_side - 2 * margin), (0...]
    pallas_call x0 -> x8, Pallas kernels: none -> 54.5 us  [the longest x7 53.2 us: call(): pl.pallas_call(kernel, out_shape=[jax.ShapeDtypeStruct(shape, kind) for s...]
  transfers between devices with their start and end apart: 24 -> 26, of which waited for: 18 -> 21; matrix products, arithmetic and copies ran while one was open for 5% -> 0% of each run, Pallas kernels for 0% -> 0%
where the time goes in v1:
time: 233 us; the launch traced here: 232 us
  starting transfers between devices  95.6 us (41%)
  Pallas kernels  54.5 us (23%)
  waiting for transfers between devices  46.6 us (20%)
  blocking collectives  27.9 us (12%)
  local copies, waits for them, and re-layouts  6.23 us (3%)
    pallas_call x7, Pallas kernels, call(): pl.pallas_call(kernel, out_shape=[jax.ShapeDtypeStruct(shape, kind) for s...  53.2 us
    ppermute x6, starting transfers between devices, total_sum(): value = value + lax.ppermute(value, axis, [(1, 2), (2, 1), (3, 0), (0, 3)])  47.7 us
    all_to_all x1, blocking collectives, body(): lax.all_to_all(sent.reshape(N_TX, CAP, SLOT_ROWS, 128), TX, split_axis=0,...  27.9 us
    ppermute x12, starting transfers between devices, shift(): return lax.ppermute(value, axes, pairs)  20.8 us
    ppermute x12, waiting for transfers between devices, shift(): return lax.ppermute(value, axes, pairs)  18.8 us
    ppermute x6, starting transfers between devices, total_sum(): value = value + lax.ppermute(value, axis, [(0, 1), (1, 0), (2, 3), (3, 2)])  17 us
    ppermute x6, waiting for transfers between devices, total_sum(): value = value + lax.ppermute(value, axis, [(1, 2), (2, 1), (3, 0), (0, 3)])  16.5 us
    ppermute x2, starting transfers between devices, total_sum(): value = value + lax.ppermute(value, 'ty_1', [(0, 1), (1, 0)])  10 us
  transfers between devices with their start and end apart: 26, of which 21 were waited for; matrix products, arithmetic and copies ran while one was open for 0% of the time, Pallas kernels for 0%

profile of v1, /device:TPU:0, one launch (start us, length us, event | category | flops | bytes accessed | tf_op | source)
XLA Modules:
  0.0 232.5 jit_solution(5599054822268616928)
XLA Ops:
  4.7 1.3 pack.1
  6.0 27.9 %all_to_all.5 = bf16[16,2,160,128]{3,2,1,0:T(8,128)(2,1)S(1)} all-to-all(bf16[16,2,160,128]{3,2,1,0:T(8,128)(2,1)S(1)} %bitcast.7), channel_id=1, replica_groups=mesh['ty_0'=4,'ty_1'=2,'tx_0'=4,'tx_1'=4] {'tx_0','tx_1'}, dimensions={0} | all-to-all | bytes 2621440 | tf_op jit(solution)/shard_map/all_to_all | solution.py:518
  34.5 7.7 %right_side.1 = (f32[544,640]{1,0:T(8,128)S(1)}, f32[32,640]{1,0:T(8,128)S(1)}, f32[32,640]{1,0:T(8,128)S(1)}, f32[32,640]{1,0:T(8,128)S(1)}, f32[32,640]{1,0:T(8,128)S(1)}, /*index=5*/bf16[32,2,256,256]{3,2,1,0:T(8,128)(2,1)}) custom-call(s32[32]{0:T(128)S(1)} %fusion.cells, bf16[32,160,128]{2,1,0:T(8,128)(2,1)S(1)} %bitcast.6), custom_call_target="tpu_custom_call" | custom-call | tf_op jit(solution)/shard_map/right_side/pallas_call | solution.py:451
  42.3 2.5 %collective-permute-start = (f32[32,640]{1,0:T(8,128)S(1)}, f32[32,640]{1,0:T(8,128)S(1)}, u32[]{:S(2)}, u32[]{:S(2)}) collective-permute-start(f32[32,640]{1,0:T(8,128)S(1)} %get-tuple-element.30), channel_id=1, source_target_pairs={{0,1},{1,2},{2,3},{3,4},{4,5},{5,6},{6,7},{7,8},{8,9},{9,10},{10,1... | collective-permute-start | bytes 245768 | tf_op jit(solution)/shard_map/ppermute | solution.py:488
  44.8 1.3 collective-permute-start.1
  46.8 4.3 %collective-permute-done.1.from_right.rim_r = f32[32,640]{1,0:T(8,128)S(1)} collective-permute-done((f32[32,640]{1,0:T(8,128)S(1)}, f32[32,640]{1,0:T(8,128)S(1)}, u32[]{:S(2)}, u32[]{:S(2)}) %collective-permute-start.1) | collective-permute-done | bytes 81952 | tf_op jit(solution)/shard_map/ppermute | solution.py:488
  51.2 1.3 collective-permute-start.2
  52.5 1.3 collective-permute-start.3
  53.9 3.7 %collective-permute-done.3.rim_b = f32[32,640]{1,0:T(8,128)S(1)} collective-permute-done((f32[32,640]{1,0:T(8,128)S(1)}, f32[32,640]{1,0:T(8,128)S(1)}, u32[]{:S(2)}, u32[]{:S(2)}) %collective-permute-start.3) | collective-permute-done | bytes 81952 | tf_op jit(solution)/shard_map/ppermute | solution.py:488
  57.6 20.2 %first_pass.1 = (f32[544,640]{1,0:T(8,128)S(1)}, f32[32,640]{1,0:T(8,128)S(1)}, f32[32,640]{1,0:T(8,128)S(1)}, f32[32,640]{1,0:T(8,128)S(1)}, f32[32,640]{1,0:T(...) custom-call(s32[32]{0:T(128)S(1)} %fusion.cells, s32[2]{0:T(128)S(1)} %pad_add_fusion.place, ...), custom_call_target="tpu_custom_call" | custom-call | tf_op jit(solution)/shard_map/first_pass/pallas_call | solution.py:451
  77.8 1.1 copy-done
  78.9 1.1 copy-done.2
  80.0 3.9 %collective-permute-start.11 = (f32[32,640]{1,0:T(8,128)S(1)}, f32[32,640]{1,0:T(8,128)S(1)}, u32[]{:S(2)}, u32[]{:S(2)}) collective-permute-start(f32[32,640]{1,0:T(8,128)S(1)} %get-tuple-element.39), channel_id=1, source_target_pairs={{0,1},{1,2},{2,3},{3,4},{4,5},{5,6},{6,7},{7,8},{8,9},{9,10},{10,1... | collective-permute-start | bytes 245768 | tf_op jit(solution)/shard_map/ppermute | solution.py:488
  83.9 1.3 collective-permute-start.12
  86.0 4.3 %collective-permute-done.12.from_right.rim_r = f32[32,640]{1,0:T(8,128)S(1)} collective-permute-done((f32[32,640]{1,0:T(8,128)S(1)}, f32[32,640]{1,0:T(8,128)S(1)}, u32[]{:S(2)}, u32[]{:S(2)}) %collective-permute-start.12) | collective-permute-done | bytes 81952 | tf_op jit(solution)/shard_map/ppermute | solution.py:488
  90.3 2.8 %collective-permute-start.13 = (f32[32,640]{1,0:T(8,128)S(1)}, f32[32,640]{1,0:T(8,128)S(1)}, u32[]{:S(2)}, u32[]{:S(2)}) collective-permute-start(f32[32,640]{1,0:T(8,128)S(1)} %get-tuple-element.43), channel_id=1, source_target_pairs={{0,16},{16,32},{32,48},{48,64},{64,80},{80,96},{96,112},{1,17},{17... | collective-permute-start | bytes 245768 | tf_op jit(solution)/shard_map/ppermute | solution.py:488
  93.1 1.3 collective-permute-start.14
  94.4 4.8 %collective-permute-start.4 = (f32[8,128]{1,0:T(8,128)S(1)}, f32[8,128]{1,0:T(8,128)S(1)}, u32[]{:S(2)}, u32[]{:S(2)}) collective-permute-start(f32[8,128]{1,0:T(8,128)S(1)} %get-tuple-element.37), channel_id=1, source_target_pairs={{0,16},{16,0},{1,17},{17,1},{2,18},{18,2},{3,19},{19,3},{4,20},{20... | collective-permute-start | bytes 12296 | tf_op jit(solution)/shard_map/ppermute | solution.py:508
  100.0 5.6 %collective-permute-start.5 = (f32[8,128]{1,0:T(8,128)S(1)}, f32[8,128]{1,0:T(8,128)S(1)}, u32[]{:S(2)}, u32[]{:S(2)}) collective-permute-start(f32[8,128]{1,0:T(8,128)S(1)} %add.50), channel_id=1, source_target_pairs={{0,1},{1,0},{2,3},{3,2},{4,5},{5,4},{6,7},{7,6},{8,9},{9,8},{10,11... | collective-permute-start | bytes 12296 | tf_op jit(solution)/shard_map/ppermute | solution.py:510
  105.6 1.6 collective-permute-done.5
  107.2 23.0 %collective-permute-start.6 = (f32[8,128]{1,0:T(8,128)S(1)}, f32[8,128]{1,0:T(8,128)S(1)}, u32[]{:S(2)}, u32[]{:S(2)}) collective-permute-start(f32[8,128]{1,0:T(8,128)S(1)} %add.51), channel_id=1, source_target_pairs={{1,2},{2,1},{3,0},{0,3},{5,6},{6,5},{7,4},{4,7},{9,10},{10,9},{11,... | collective-permute-start | bytes 12296 | tf_op jit(solution)/shard_map/ppermute | solution.py:511
  130.2 1.6 collective-permute-done.6
  131.8 2.9 %collective-permute-start.7 = (f32[8,128]{1,0:T(8,128)S(1)}, f32[8,128]{1,0:T(8,128)S(1)}, u32[]{:S(2)}, u32[]{:S(2)}) collective-permute-start(f32[8,128]{1,0:T(8,128)S(1)} %add.52), channel_id=1, source_target_pairs={{0,4},{4,0},{8,12},{12,8},{1,5},{5,1},{9,13},{13,9},{2,6},{6,2},{1... | collective-permute-start | bytes 12296 | tf_op jit(solution)/shard_map/ppermute | solution.py:510
  134.7 1.6 collective-permute-done.7
  136.3 4.8 %collective-permute-done.8 = f32[8,128]{1,0:T(8,128)S(1)} collective-permute-done((f32[8,128]{1,0:T(8,128)S(1)}, f32[8,128]{1,0:T(8,128)S(1)}, u32[]{:S(2)}, u32[]{:S(2)}) %collective-permute-start.8) | collective-permute-done | bytes 4128 | tf_op jit(solution)/shard_map/ppermute | solution.py:511
  141.1 2.0 collective-permute-start.9
  143.1 1.6 collective-permute-done.9
  144.7 2.7 %collective-permute-start.10 = (f32[8,128]{1,0:T(8,128)S(1)}, f32[8,128]{1,0:T(8,128)S(1)}, u32[]{:S(2)}, u32[]{:S(2)}) collective-permute-start(f32[8,128]{1,0:T(8,128)S(1)} %add.55), channel_id=1, source_target_pairs={{32,64},{64,32},{96,0},{0,96},{33,65},{65,33},{97,1},{1,97},{34,66... | collective-permute-start | bytes 12296 | tf_op jit(solution)/shard_map/ppermute | solution.py:511
  147.4 2.1 collective-permute-done.10
  149.6 22.0 %second_pass.1 = (f32[544,640]{1,0:T(8,128)S(1)}, f32[32,640]{1,0:T(8,128)S(1)}, f32[32,640]{1,0:T(8,128)S(1)}, f32[32,640]{1,0:T(8,128)S(1)}, f32[32,640]{1,0:T...) custom-call(s32[32]{0:T(128)S(1)} %fusion.cells, s32[2]{0:T(128)S(1)} %pad_add_fusion.place, ...), custom_call_target="tpu_custom_call" | custom-call | tf_op jit(solution)/shard_map/second_pass/pallas_call | solution.py:451
  171.6 1.3 collective-permute-start.22
  172.9 1.3 collective-permute-start.23
  174.9 4.3 %collective-permute-done.23.from_right.rim_r = f32[32,640]{1,0:T(8,128)S(1)} collective-permute-done((f32[32,640]{1,0:T(8,128)S(1)}, f32[32,640]{1,0:T(8,128)S(1)}, u32[]{:S(2)}, u32[]{:S(2)}) %collective-permute-start.23) | collective-permute-done | bytes 81952 | tf_op jit(solution)/shard_map/ppermute | solution.py:488
  179.3 1.3 collective-permute-start.24
  180.6 1.3 collective-permute-start.25
  181.9 5.2 %collective-permute-start.15 = (f32[8,128]{1,0:T(8,128)S(1)}, f32[8,128]{1,0:T(8,128)S(1)}, u32[]{:S(2)}, u32[]{:S(2)}) collective-permute-start(f32[8,128]{1,0:T(8,128)S(1)} %get-tuple-element.46), channel_id=1, source_target_pairs={{0,16},{16,0},{1,17},{17,1},{2,18},{18,2},{3,19},{19,3},{4,20},{20... | collective-permute-start | bytes 12296 | tf_op jit(solution)/shard_map/ppermute | solution.py:508
  188.0 2.0 collective-permute-start.16
  190.0 1.6 collective-permute-done.16
  191.6 18.2 %collective-permute-start.17 = (f32[8,128]{1,0:T(8,128)S(1)}, f32[8,128]{1,0:T(8,128)S(1)}, u32[]{:S(2)}, u32[]{:S(2)}) collective-permute-start(f32[8,128]{1,0:T(8,128)S(1)} %add.58), channel_id=1, source_target_pairs={{1,2},{2,1},{3,0},{0,3},{5,6},{6,5},{7,4},{4,7},{9,10},{10,9},{11,... | collective-permute-start | bytes 12296 | tf_op jit(solution)/shard_map/ppermute | solution.py:511
  209.8 1.6 collective-permute-done.17
  211.3 2.6 %collective-permute-start.18 = (f32[8,128]{1,0:T(8,128)S(1)}, f32[8,128]{1,0:T(8,128)S(1)}, u32[]{:S(2)}, u32[]{:S(2)}) collective-permute-start(f32[8,128]{1,0:T(8,128)S(1)} %add.59), channel_id=1, source_target_pairs={{0,4},{4,0},{8,12},{12,8},{1,5},{5,1},{9,13},{13,9},{2,6},{6,2},{1... | collective-permute-start | bytes 12296 | tf_op jit(solution)/shard_map/ppermute | solution.py:510
  213.9 1.6 collective-permute-done.18
  215.5 4.8 %collective-permute-done.19 = f32[8,128]{1,0:T(8,128)S(1)} collective-permute-done((f32[8,128]{1,0:T(8,128)S(1)}, f32[8,128]{1,0:T(8,128)S(1)}, u32[]{:S(2)}, u32[]{:S(2)}) %collective-permute-start.19) | collective-permute-done | bytes 4128 | tf_op jit(solution)/shard_map/ppermute | solution.py:511
  220.3 2.0 collective-permute-start.20
  222.3 1.6 collective-permute-done.20
  223.9 3.9 %collective-permute-start.21 = (f32[8,128]{1,0:T(8,128)S(1)}, f32[8,128]{1,0:T(8,128)S(1)}, u32[]{:S(2)}, u32[]{:S(2)}) collective-permute-start(f32[8,128]{1,0:T(8,128)S(1)} %add.62), channel_id=1, source_target_pairs={{32,64},{64,32},{96,0},{0,96},{33,65},{65,33},{97,1},{1,97},{34,66... | collective-permute-start | bytes 12296 | tf_op jit(solution)/shard_map/ppermute | solution.py:511
  227.9 1.6 collective-permute-done.21
  229.5 3.0 %finish.1 = (f32[512,512]{1,0:T(8,128)}, f32[512,512]{1,0:T(8,128)}) custom-call(s32[2]{0:T(128)S(1)} %pad_add_fusion.place, f32[8,128]{1,0:T(8,128)S(1)} %add.56.sums_in.sums_one, f32[8,128]{1,0:T(8,128)S(1)} %add.63.sums_two, f32[544,640]{1,0:T(8,128)S(1)} %get-tuple-element.47.own_in, f32[32,640]{1,0:T(8,128)S(1)} %collective-permute-done.22.from_left.rim_l, ...), custom_call_target="tpu_custom_call" | custom-call | tf_op jit(solution)/shard_map/finish/pallas_call | solution.py:451
  (43 shorter events, 8.9 us)
Async XLA Ops:
  2.3 1.0 copy-start.3
  3.4 0.7 copy-start.4
  4.0 0.7 copy-start.5
  42.3 4.5 %collective-permute-start = (f32[32,640]{1,0:T(8,128)S(1)}, f32[32,640]{1,0:T(8,128)S(1)}, u32[]{:S(2)}, u32[]{:S(2)}) collective-permute-start(f32[32,640]{1,0:T(8,128)S(1)} %get-tuple-element.30), channel_id=1, source_target_pairs={{0,1},{1,2},{2,3},{3,4},{4,5},{5,6},{6,7},{7,8},{8,9},{9,10},{10,1... | collective-permute-start | bytes 245768 | tf_op jit(solution)/shard_map/ppermute | solution.py:488
  44.8 6.3 %collective-permute-start.1 = (f32[32,640]{1,0:T(8,128)S(1)}, f32[32,640]{1,0:T(8,128)S(1)}, u32[]{:S(2)}, u32[]{:S(2)}) collective-permute-start(f32[32,640]{1,0:T(8,128)S(1)} %get-tuple-element.31), channel_id=1, source_target_pairs={{1,0},{2,1},{3,2},{4,3},{5,4},{6,5},{7,6},{8,7},{9,8},{10,9},{11,1... | collective-permute-start | bytes 245768 | tf_op jit(solution)/shard_map/ppermute | solution.py:488
  51.2 2.7 %collective-permute-start.2 = (f32[32,640]{1,0:T(8,128)S(1)}, f32[32,640]{1,0:T(8,128)S(1)}, u32[]{:S(2)}, u32[]{:S(2)}) collective-permute-start(f32[32,640]{1,0:T(8,128)S(1)} %get-tuple-element.34), channel_id=1, source_target_pairs={{0,16},{16,32},{32,48},{48,64},{64,80},{80,96},{96,112},{1,17},{17... | collective-permute-start | bytes 245768 | tf_op jit(solution)/shard_map/ppermute | solution.py:488
  52.5 5.1 %collective-permute-start.3 = (f32[32,640]{1,0:T(8,128)S(1)}, f32[32,640]{1,0:T(8,128)S(1)}, u32[]{:S(2)}, u32[]{:S(2)}) collective-permute-start(f32[32,640]{1,0:T(8,128)S(1)} %get-tuple-element.35), channel_id=1, source_target_pairs={{16,0},{32,16},{48,32},{64,48},{80,64},{96,80},{112,96},{17,1},{33... | collective-permute-start | bytes 245768 | tf_op jit(solution)/shard_map/ppermute | solution.py:488
  77.8 1.1 copy-start
  78.9 1.1 copy-start.2
  80.0 5.9 %collective-permute-start.11 = (f32[32,640]{1,0:T(8,128)S(1)}, f32[32,640]{1,0:T(8,128)S(1)}, u32[]{:S(2)}, u32[]{:S(2)}) collective-permute-start(f32[32,640]{1,0:T(8,128)S(1)} %get-tuple-element.39), channel_id=1, source_target_pairs={{0,1},{1,2},{2,3},{3,4},{4,5},{5,6},{6,7},{7,8},{8,9},{9,10},{10,1... | collective-permute-start | bytes 245768 | tf_op jit(solution)/shard_map/ppermute | solution.py:488
  83.9 6.3 %collective-permute-start.12 = (f32[32,640]{1,0:T(8,128)S(1)}, f32[32,640]{1,0:T(8,128)S(1)}, u32[]{:S(2)}, u32[]{:S(2)}) collective-permute-start(f32[32,640]{1,0:T(8,128)S(1)} %get-tuple-element.40), channel_id=1, source_target_pairs={{1,0},{2,1},{3,2},{4,3},{5,4},{6,5},{7,6},{8,7},{9,8},{10,9},{11,1... | collective-permute-start | bytes 245768 | tf_op jit(solution)/shard_map/ppermute | solution.py:488
  90.3 59.2 %collective-permute-start.13 = (f32[32,640]{1,0:T(8,128)S(1)}, f32[32,640]{1,0:T(8,128)S(1)}, u32[]{:S(2)}, u32[]{:S(2)}) collective-permute-start(f32[32,640]{1,0:T(8,128)S(1)} %get-tuple-element.43), channel_id=1, source_target_pairs={{0,16},{16,32},{32,48},{48,64},{64,80},{80,96},{96,112},{1,17},{17... | collective-permute-start | bytes 245768 | tf_op jit(solution)/shard_map/ppermute | solution.py:488
  93.1 56.4 %collective-permute-start.14 = (f32[32,640]{1,0:T(8,128)S(1)}, f32[32,640]{1,0:T(8,128)S(1)}, u32[]{:S(2)}, u32[]{:S(2)}) collective-permute-start(f32[32,640]{1,0:T(8,128)S(1)} %get-tuple-element.44), channel_id=1, source_target_pairs={{16,0},{32,16},{48,32},{64,48},{80,64},{96,80},{112,96},{17,1},{33... | collective-permute-start | bytes 245768 | tf_op jit(solution)/shard_map/ppermute | solution.py:488
  94.4 5.6 %collective-permute-start.4 = (f32[8,128]{1,0:T(8,128)S(1)}, f32[8,128]{1,0:T(8,128)S(1)}, u32[]{:S(2)}, u32[]{:S(2)}) collective-permute-start(f32[8,128]{1,0:T(8,128)S(1)} %get-tuple-element.37), channel_id=1, source_target_pairs={{0,16},{16,0},{1,17},{17,1},{2,18},{18,2},{3,19},{19,3},{4,20},{20... | collective-permute-start | bytes 12296 | tf_op jit(solution)/shard_map/ppermute | solution.py:508
  100.0 7.2 %collective-permute-start.5 = (f32[8,128]{1,0:T(8,128)S(1)}, f32[8,128]{1,0:T(8,128)S(1)}, u32[]{:S(2)}, u32[]{:S(2)}) collective-permute-start(f32[8,128]{1,0:T(8,128)S(1)} %add.50), channel_id=1, source_target_pairs={{0,1},{1,0},{2,3},{3,2},{4,5},{5,4},{6,7},{7,6},{8,9},{9,8},{10,11... | collective-permute-start | bytes 12296 | tf_op jit(solution)/shard_map/ppermute | solution.py:510
  107.2 24.6 %collective-permute-start.6 = (f32[8,128]{1,0:T(8,128)S(1)}, f32[8,128]{1,0:T(8,128)S(1)}, u32[]{:S(2)}, u32[]{:S(2)}) collective-permute-start(f32[8,128]{1,0:T(8,128)S(1)} %add.51), channel_id=1, source_target_pairs={{1,2},{2,1},{3,0},{0,3},{5,6},{6,5},{7,4},{4,7},{9,10},{10,9},{11,... | collective-permute-start | bytes 12296 | tf_op jit(solution)/shard_map/ppermute | solution.py:511
  131.8 4.5 %collective-permute-start.7 = (f32[8,128]{1,0:T(8,128)S(1)}, f32[8,128]{1,0:T(8,128)S(1)}, u32[]{:S(2)}, u32[]{:S(2)}) collective-permute-start(f32[8,128]{1,0:T(8,128)S(1)} %add.52), channel_id=1, source_target_pairs={{0,4},{4,0},{8,12},{12,8},{1,5},{5,1},{9,13},{13,9},{2,6},{6,2},{1... | collective-permute-start | bytes 12296 | tf_op jit(solution)/shard_map/ppermute | solution.py:510
  136.3 4.8 %collective-permute-start.8 = (f32[8,128]{1,0:T(8,128)S(1)}, f32[8,128]{1,0:T(8,128)S(1)}, u32[]{:S(2)}, u32[]{:S(2)}) collective-permute-start(f32[8,128]{1,0:T(8,128)S(1)} %add.53), channel_id=1, source_target_pairs={{4,8},{8,4},{12,0},{0,12},{5,9},{9,5},{13,1},{1,13},{6,10},{10,6},... | collective-permute-start | bytes 12296 | tf_op jit(solution)/shard_map/ppermute | solution.py:511
  141.1 3.6 %collective-permute-start.9 = (f32[8,128]{1,0:T(8,128)S(1)}, f32[8,128]{1,0:T(8,128)S(1)}, u32[]{:S(2)}, u32[]{:S(2)}) collective-permute-start(f32[8,128]{1,0:T(8,128)S(1)} %add.54), channel_id=1, source_target_pairs={{0,32},{32,0},{64,96},{96,64},{1,33},{33,1},{65,97},{97,65},{2,34}... | collective-permute-start | bytes 12296 | tf_op jit(solution)/shard_map/ppermute | solution.py:510
  144.7 4.8 %collective-permute-start.10 = (f32[8,128]{1,0:T(8,128)S(1)}, f32[8,128]{1,0:T(8,128)S(1)}, u32[]{:S(2)}, u32[]{:S(2)}) collective-permute-start(f32[8,128]{1,0:T(8,128)S(1)} %add.55), channel_id=1, source_target_pairs={{32,64},{64,32},{96,0},{0,96},{33,65},{65,33},{97,1},{1,97},{34,66... | collective-permute-start | bytes 12296 | tf_op jit(solution)/shard_map/ppermute | solution.py:511
  149.6 79.9 %copy-start.1 = (f32[544,640]{1,0:T(8,128)S(1)}, f32[544,640]{1,0:T(8,128)}, u32[]{:S(2)}) copy-start(f32[544,640]{1,0:T(8,128)} %copy-done) | copy-start | bytes 4177924
  171.6 3.3 %collective-permute-start.22 = (f32[32,640]{1,0:T(8,128)S(1)}, f32[32,640]{1,0:T(8,128)S(1)}, u32[]{:S(2)}, u32[]{:S(2)}) collective-permute-start(f32[32,640]{1,0:T(8,128)S(1)} %get-tuple-element.48), channel_id=1, source_target_pairs={{0,1},{1,2},{2,3},{3,4},{4,5},{5,6},{6,7},{7,8},{8,9},{9,10},{10,1... | collective-permute-start | bytes 245768 | tf_op jit(solution)/shard_map/ppermute | solution.py:488
  172.9 6.3 %collective-permute-start.23 = (f32[32,640]{1,0:T(8,128)S(1)}, f32[32,640]{1,0:T(8,128)S(1)}, u32[]{:S(2)}, u32[]{:S(2)}) collective-permute-start(f32[32,640]{1,0:T(8,128)S(1)} %get-tuple-element.49), channel_id=1, source_target_pairs={{1,0},{2,1},{3,2},{4,3},{5,4},{6,5},{7,6},{8,7},{9,8},{10,9},{11,1... | collective-permute-start | bytes 245768 | tf_op jit(solution)/shard_map/ppermute | solution.py:488
  179.3 50.1 %collective-permute-start.24 = (f32[32,640]{1,0:T(8,128)S(1)}, f32[32,640]{1,0:T(8,128)S(1)}, u32[]{:S(2)}, u32[]{:S(2)}) collective-permute-start(f32[32,640]{1,0:T(8,128)S(1)} %get-tuple-element.52), channel_id=1, source_target_pairs={{0,16},{16,32},{32,48},{48,64},{64,80},{80,96},{96,112},{1,17},{17... | collective-permute-start | bytes 245768 | tf_op jit(solution)/shard_map/ppermute | solution.py:488
  180.6 48.8 %collective-permute-start.25 = (f32[32,640]{1,0:T(8,128)S(1)}, f32[32,640]{1,0:T(8,128)S(1)}, u32[]{:S(2)}, u32[]{:S(2)}) collective-permute-start(f32[32,640]{1,0:T(8,128)S(1)} %get-tuple-element.53), channel_id=1, source_target_pairs={{16,0},{32,16},{48,32},{64,48},{80,64},{96,80},{112,96},{17,1},{33... | collective-permute-start | bytes 245768 | tf_op jit(solution)/shard_map/ppermute | solution.py:488
  181.9 6.1 %collective-permute-start.15 = (f32[8,128]{1,0:T(8,128)S(1)}, f32[8,128]{1,0:T(8,128)S(1)}, u32[]{:S(2)}, u32[]{:S(2)}) collective-permute-start(f32[8,128]{1,0:T(8,128)S(1)} %get-tuple-element.46), channel_id=1, source_target_pairs={{0,16},{16,0},{1,17},{17,1},{2,18},{18,2},{3,19},{19,3},{4,20},{20... | collective-permute-start | bytes 12296 | tf_op jit(solution)/shard_map/ppermute | solution.py:508
  188.0 3.6 %collective-permute-start.16 = (f32[8,128]{1,0:T(8,128)S(1)}, f32[8,128]{1,0:T(8,128)S(1)}, u32[]{:S(2)}, u32[]{:S(2)}) collective-permute-start(f32[8,128]{1,0:T(8,128)S(1)} %add.57), channel_id=1, source_target_pairs={{0,1},{1,0},{2,3},{3,2},{4,5},{5,4},{6,7},{7,6},{8,9},{9,8},{10,11... | collective-permute-start | bytes 12296 | tf_op jit(solution)/shard_map/ppermute | solution.py:510
  191.6 19.7 %collective-permute-start.17 = (f32[8,128]{1,0:T(8,128)S(1)}, f32[8,128]{1,0:T(8,128)S(1)}, u32[]{:S(2)}, u32[]{:S(2)}) collective-permute-start(f32[8,128]{1,0:T(8,128)S(1)} %add.58), channel_id=1, source_target_pairs={{1,2},{2,1},{3,0},{0,3},{5,6},{6,5},{7,4},{4,7},{9,10},{10,9},{11,... | collective-permute-start | bytes 12296 | tf_op jit(solution)/shard_map/ppermute | solution.py:511
  211.3 4.2 %collective-permute-start.18 = (f32[8,128]{1,0:T(8,128)S(1)}, f32[8,128]{1,0:T(8,128)S(1)}, u32[]{:S(2)}, u32[]{:S(2)}) collective-permute-start(f32[8,128]{1,0:T(8,128)S(1)} %add.59), channel_id=1, source_target_pairs={{0,4},{4,0},{8,12},{12,8},{1,5},{5,1},{9,13},{13,9},{2,6},{6,2},{1... | collective-permute-start | bytes 12296 | tf_op jit(solution)/shard_map/ppermute | solution.py:510
  215.5 4.8 %collective-permute-start.19 = (f32[8,128]{1,0:T(8,128)S(1)}, f32[8,128]{1,0:T(8,128)S(1)}, u32[]{:S(2)}, u32[]{:S(2)}) collective-permute-start(f32[8,128]{1,0:T(8,128)S(1)} %add.60), channel_id=1, source_target_pairs={{4,8},{8,4},{12,0},{0,12},{5,9},{9,5},{13,1},{1,13},{6,10},{10,6},... | collective-permute-start | bytes 12296 | tf_op jit(solution)/shard_map/ppermute | solution.py:511
  220.3 3.6 %collective-permute-start.20 = (f32[8,128]{1,0:T(8,128)S(1)}, f32[8,128]{1,0:T(8,128)S(1)}, u32[]{:S(2)}, u32[]{:S(2)}) collective-permute-start(f32[8,128]{1,0:T(8,128)S(1)} %add.61), channel_id=1, source_target_pairs={{0,32},{32,0},{64,96},{96,64},{1,33},{33,1},{65,97},{97,65},{2,34}... | collective-permute-start | bytes 12296 | tf_op jit(solution)/shard_map/ppermute | solution.py:510
  223.9 5.5 %collective-permute-start.21 = (f32[8,128]{1,0:T(8,128)S(1)}, f32[8,128]{1,0:T(8,128)S(1)}, u32[]{:S(2)}, u32[]{:S(2)}) collective-permute-start(f32[8,128]{1,0:T(8,128)S(1)} %add.62), channel_id=1, source_target_pairs={{32,64},{64,32},{96,0},{0,96},{33,65},{65,33},{97,1},{1,97},{34,66... | collective-permute-start | bytes 12296 | tf_op jit(solution)/shard_map/ppermute | solution.py:511
